TPU v7x, 128 devices: a whole 4x4x4 slice. The times are simulated.
128 devices in a mesh: ta: 8 (over z, core), af: 16 (over x, y).
Axes of the slice: x: 4, y: 4, z: 4, core: 2. Of those that a mesh axis runs over, the one named last changes fastest.
Arguments:
- velocity: float32 [16, 512, 128, 128], P(None, ('ta', 'af')), may hold values from -14 to 14
- initial_basis: float32 [512, 64], replicated, may hold values from -6 to 6
Outputs:
- core: float32 [16, 128, 64, 128], P('ta', 'af')
All inputs are finite; a program needn't handle non-finite values.
Results may differ from a plain program's by a relative error of at most 0.00017.
Values sent between devices are 32-bit elements; how exact they have to be, the bound alone decides.
A program may use at most 64 MiB of HBM per device.

v0:
```python
import jax
import jax.numpy as jnp
from jax import lax
from jax.sharding import PartitionSpec as P

ITERS = 3


def orthonormal(product):
    lower = jnp.linalg.cholesky(
        jnp.dot(
            product.T, product, precision=lax.Precision.HIGHEST, preferred_element_type=jnp.float32
        )
    )
    return jax.scipy.linalg.solve_triangular(lower, product.T, lower=True).T


def local(velocity, initial_basis):
    groups_ta = lax.axis_size("ta")
    groups_af = lax.axis_size("af")
    frames, slab_planes, cells_x, cells_y = velocity.shape
    planes_total = initial_basis.shape[0]
    blocked = velocity.reshape(
        groups_ta, frames // groups_ta, slab_planes, groups_af, cells_x // groups_af, cells_y
    )
    blocked = blocked.transpose(0, 3, 1, 2, 4, 5).reshape(
        groups_ta * groups_af, frames // groups_ta, slab_planes, cells_x // groups_af, cells_y
    )
    fibres = lax.all_to_all(blocked, ("ta", "af"), split_axis=0, concat_axis=2, tiled=True)
    fibres = fibres.reshape(frames // groups_ta, planes_total, cells_x // groups_af, cells_y)
    gram_local = jnp.einsum(
        "fzxy,fwxy->zw",
        fibres,
        fibres,
        precision=lax.Precision.HIGHEST,
        preferred_element_type=jnp.float32,
    )
    gram_matrix = lax.psum(gram_local, ("ta", "af"))
    subspace = initial_basis
    for iteration in range(ITERS):
        subspace = orthonormal(
            jnp.dot(
                gram_matrix,
                subspace,
                precision=lax.Precision.HIGHEST,
                preferred_element_type=jnp.float32,
            )
        )
    return jnp.einsum(
        "fzxy,zk->fxky",
        fibres,
        subspace,
        precision=lax.Precision.HIGHEST,
        preferred_element_type=jnp.float32,
    )


def solution(mesh):
    placed = (P(None, ("ta", "af"), None, None), P())
    return jax.shard_map(
        local, mesh=mesh, in_specs=placed, out_specs=P("ta", "af", None, None), check_vma=False
    )
```

profile of v0, /device:TPU:1, one launch (start us, length us, event | category | flops | bytes accessed | tf_op | source)
XLA Modules:
  0.0 287.6 jit_solution(15660621444785246462)
XLA Ops:
  6.5 5.0 %copy.7 = f32[8,2,4,16,8,128]{5,2,4,1,3,0:T(4,128)S(1)} copy(f32[8,2,4,16,8,128]{5,4,3,2,1,0:T(8,128)} %bitcast.74) | data formatting | bytes 8388608 | tf_op jit(solution)/shard_map/reshape | solution.py:23
  11.5 64.0 %all_to_all.15 = f32[128,2,4,8,128]{4,2,3,1,0:T(4,128)S(1)} all-to-all(f32[128,2,4,8,128]{4,2,3,1,0:T(4,128)S(1)} %bitcast.73), channel_id=1, replica_groups=mesh['ta'=8,'af'=16] {'ta','af'}, dimensions={0} | all-to-all | bytes 8388608 | tf_op jit(solution)/shard_map/all_to_all | solution.py:29
  75.5 1.0 copy.8
  76.5 1.9 copy-done.1
  78.4 7.9 %convolution_bitcast_fusion = f32[512,512]{1,0:T(8,128)} fusion(f32[2,512,8,128]{3,1,2,0:T(8,128)S(1)} %bitcast.70), kind=kOutput, calls=%fused_computation | convolution fusion | flops 6442450944 | bytes 5242880 | tf_op jit(solution)/shard_map/fzxy,fwxy->zw/dot_general | solution.py:31
  86.3 0.0 all-reduce.2.cloned.1.call-update
  86.3 144.4 %all-reduce.2.cloned.1.call-done = f32[512,512]{1,0:T(8,128)} async-done(((f32[512,512]{1,0:T(8,128)}), f32[512,512]{1,0:T(8,128)}) %all-reduce.2.cloned.1.call-update) | async-done | bytes 1048592 | tf_op jit(solution)/shard_map/psum | solution.py:38
  230.7 2.4 fusion.18
  233.2 0.3 fusion.19
  233.4 0.1 copy.9
  233.5 5.8 %cholesky.59 = f32[64,64]{1,0:T(8,128)S(1)} custom-call(f32[64,64]{1,0:T(8,128)S(1)} %fusion.13), custom_call_target="Cholesky" | custom-call | tf_op jit(solution)/shard_map/jit(cholesky)/cholesky | solution.py:10
  239.4 0.6 compare_reduce_fusion.2
  240.1 0.7 fusion.5
  240.7 4.9 %custom-call.7 = f32[1,64,64]{1,2,0:T(8,128)S(1)} custom-call(f32[1,64,64]{2,1,0:T(8,128)S(1)} %fusion.5), custom_call_target="InvertDiagBlocksLowerTriangular" | custom-call | tf_op jit(solution)/shard_map/jit(_solve_triangular)/triangular_solve | solution.py:15
  245.6 0.3 fusion.3
  246.0 2.4 fusion.20
  248.3 0.3 fusion.21
  248.6 0.1 copy.10
  248.7 6.0 %cholesky.70 = f32[64,64]{1,0:T(8,128)S(1)} custom-call(f32[64,64]{1,0:T(8,128)S(1)} %fusion.11), custom_call_target="Cholesky" | custom-call | tf_op jit(solution)/shard_map/jit(cholesky)/cholesky | solution.py:10
  254.7 0.6 compare_reduce_fusion.1
  255.4 0.7 fusion.6
  256.0 4.9 %custom-call.8 = f32[1,64,64]{1,2,0:T(8,128)S(1)} custom-call(f32[1,64,64]{2,1,0:T(8,128)S(1)} %fusion.6), custom_call_target="InvertDiagBlocksLowerTriangular" | custom-call | tf_op jit(solution)/shard_map/jit(_solve_triangular)/triangular_solve | solution.py:15
  260.9 0.3 fusion.1
  261.3 1.1 fusion.22
  262.4 0.3 fusion.23
  262.7 0.1 copy.11
  262.8 5.8 %cholesky.81 = f32[64,64]{1,0:T(8,128)S(1)} custom-call(f32[64,64]{1,0:T(8,128)S(1)} %fusion.9), custom_call_target="Cholesky" | custom-call | tf_op jit(solution)/shard_map/jit(cholesky)/cholesky | solution.py:10
  268.6 0.6 compare_reduce_fusion
  269.3 0.7 fusion.7
  269.9 4.9 %custom-call.9 = f32[1,64,64]{1,2,0:T(8,128)S(1)} custom-call(f32[1,64,64]{2,1,0:T(8,128)S(1)} %fusion.7), custom_call_target="InvertDiagBlocksLowerTriangular" | custom-call | tf_op jit(solution)/shard_map/jit(_solve_triangular)/triangular_solve | solution.py:15
  274.8 0.3 convolution_bitcast_fusion.2
  275.2 5.6 %convolution_bitcast_fusion.1 = f32[2,8,64,128]{3,2,1,0:T(8,128)} fusion(f32[64,512,1,1]{1,0,3,2:T(8,128)S(1)} %convolution_bitcast_fusion.2, f32[2,512,8,128]{3,1,2,0:T(8,128)} %bitcast.71), kind=kOutput, calls=%fused_computation.1 | convolution fusion | flops 805306368 | bytes 4849664 | tf_op jit(solution)/shard_map/fzxy,zk->fxky/dot_general | solution.py:49
  (12 shorter events, 0.1 us)
Async XLA Ops:
  6.5 224.2 %copy-start = (f32[512,64]{0,1:T(8,128)S(1)}, f32[512,64]{0,1:T(8,128)}, u32[]{:S(2)}) copy-start(f32[512,64]{0,1:T(8,128)} %param.6) | copy-start | bytes 393220
  6.5 224.2 %all-reduce.2.cloned.1.call-start = ((), (), s32[]{:S(2)}) async-start(), calls=%async_computation.1 | async-start | bytes 2097152 | tf_op jit(solution)/shard_map/psum | solution.py:38
  76.5 1.9 copy-start.1
  230.7 30.5 %copy-start.2 = (f32[512,512]{1,0:T(8,128)S(1)}, f32[512,512]{1,0:T(8,128)}, u32[]{:S(2)}) copy-start(f32[512,512]{1,0:T(8,128)} %all-reduce.2.cloned.1.call-done) | copy-start | bytes 3145732
Sparse Core Ops, SparseCore 0:
  86.5 144.2 all-reduce.1
where the time goes:
time: 288 us
  waiting for transfers between devices  144 us (50%)
  blocking collectives  64 us (22%)
  other arithmetic  36.4 us (13%)
  matrix products  21.3 us (7%)
  between operations  13.5 us (5%)
  local copies, waits for them, and re-layouts  8.09 us (3%)
    psum x1, waiting for transfers between devices, local(): gram_matrix = lax.psum(gram_local, ('ta', 'af'))  144 us
    all_to_all x1, blocking collectives, local(): lax.all_to_all(blocked, ('ta', 'af'), split_axis=0, concat_axis=2, tiled=...  64 us
    another operation x9, other arithmetic, orthonormal(): jnp.linalg.cholesky(jnp.dot(product.T, product, precision=lax.Precision.H...  19.7 us
    another operation x6, other arithmetic, orthonormal(): return jax.scipy.linalg.solve_triangular(lower, product.T, lower=True).T  16.6 us
    dot_general x1, matrix products, local(): jnp.einsum('fzxy,fwxy->zw', fibres, fibres, precision=lax.Precision.HIGHE...  7.93 us
    dot_general x3, matrix products, local(): jnp.dot(gram_matrix, subspace, precision=lax.Precision.HIGHEST, preferred...  5.94 us
  transfers between devices with their start and end apart: 1, of which 1 were waited for; matrix products, arithmetic and copies ran while one was open for 0% of the time, Pallas kernels for 0%

commit v1 on v0

--- a/solution.py
+++ b/solution.py
@@ -26,7 +26,10 @@
     blocked = blocked.transpose(0, 3, 1, 2, 4, 5).reshape(
         groups_ta * groups_af, frames // groups_ta, slab_planes, cells_x // groups_af, cells_y
     )
-    fibres = lax.all_to_all(blocked, ("ta", "af"), split_axis=0, concat_axis=2, tiled=True)
+    met_up = lax.all_to_all(
+        jnp.stack(jnp.split(blocked, lax.axis_size(("ta", "af")), axis=0)), ("ta", "af"), 0, 0
+    )
+    fibres = jnp.concatenate(met_up, axis=2)
     fibres = fibres.reshape(frames // groups_ta, planes_total, cells_x // groups_af, cells_y)
     gram_local = jnp.einsum(
         "fzxy,fwxy->zw",

time: 288 us -> 290 us (level)
  no operation moved by 1% of the time
where the time goes in v1:
time: 290 us
  waiting for transfers between devices  144 us (50%)
  blocking collectives  64 us (22%)
  other arithmetic  36.4 us (13%)
  matrix products  21.3 us (7%)
  between operations  14.1 us (5%)
  local copies, waits for them, and re-layouts  9.5 us (3%)
    psum x1, waiting for transfers between devices, local(): gram_matrix = lax.psum(gram_local, ('ta', 'af'))  144 us
    all_to_all x1, blocking collectives, local(): lax.all_to_all(jnp.stack(jnp.split(blocked, lax.axis_size(('ta', 'af')),...  64 us
    another operation x9, other arithmetic, orthonormal(): jnp.linalg.cholesky(jnp.dot(product.T, product, precision=lax.Precision.H...  19.7 us
    another operation x6, other arithmetic, orthonormal(): return jax.scipy.linalg.solve_triangular(lower, product.T, lower=True).T  16.6 us
    dot_general x1, matrix products, local(): jnp.einsum('fzxy,fwxy->zw', fibres, fibres, precision=lax.Precision.HIGHE...  7.93 us
    dot_general x3, matrix products, local(): jnp.dot(gram_matrix, subspace, precision=lax.Precision.HIGHEST, preferred...  5.94 us
  transfers between devices with their start and end apart: 1, of which 1 were waited for; matrix products, arithmetic and copies ran while one was open for 0% of the time, Pallas kernels for 0%

profile of v1, /device:TPU:1, one launch (start us, length us, event | category | flops | bytes accessed | tf_op | source)
XLA Modules:
  0.0 289.7 jit_solution(6423642127720284553)
XLA Ops:
  6.5 5.0 %copy.134 = f32[8,2,4,16,8,128]{5,2,4,1,3,0:T(4,128)S(1)} copy(f32[8,2,4,16,8,128]{5,4,3,2,1,0:T(8,128)} %bitcast.711) | data formatting | bytes 8388608 | tf_op jit(solution)/shard_map/reshape | solution.py:23
  13.5 64.0 %all_to_all.5 = f32[128,1,2,4,8,128]{5,3,4,2,1,0:T(4,128)S(1)} all-to-all(f32[128,1,2,4,8,128]{5,3,4,2,1,0:T(4,128)S(1)} %constant_dynamic-update-slice_fusion), channel_id=1, replica_groups=mesh['ta'=8,'af'=16] {'ta','af'}, dimensions={0} | all-to-all | bytes 8388608 | tf_op jit(solution)/shard_map/all_to_all | solution.py:29
  77.5 1.0 copy.135
  78.5 1.9 copy-done.1
  80.4 7.9 %convolution_bitcast_fusion = f32[512,512]{1,0:T(8,128)} fusion(f32[2,512,8,128]{3,1,2,0:T(8,128)S(1)} %bitcast.580), kind=kOutput, calls=%fused_computation | convolution fusion | flops 6442450944 | bytes 5242880 | tf_op jit(solution)/shard_map/fzxy,fwxy->zw/dot_general | solution.py:34
  88.3 0.0 all-reduce.2.cloned.1.call-update
  88.4 144.4 %all-reduce.2.cloned.1.call-done = f32[512,512]{1,0:T(8,128)} async-done(((f32[512,512]{1,0:T(8,128)}), f32[512,512]{1,0:T(8,128)}) %all-reduce.2.cloned.1.call-update) | async-done | bytes 1048592 | tf_op jit(solution)/shard_map/psum | solution.py:41
  232.7 2.4 fusion.18
  235.2 0.3 fusion.19
  235.5 0.1 copy.136
  235.6 5.8 %cholesky.59 = f32[64,64]{1,0:T(8,128)S(1)} custom-call(f32[64,64]{1,0:T(8,128)S(1)} %fusion.13), custom_call_target="Cholesky" | custom-call | tf_op jit(solution)/shard_map/jit(cholesky)/cholesky | solution.py:10
  241.4 0.6 compare_reduce_fusion.2
  242.1 0.7 fusion.5
  242.7 4.9 %custom-call.7 = f32[1,64,64]{1,2,0:T(8,128)S(1)} custom-call(f32[1,64,64]{2,1,0:T(8,128)S(1)} %fusion.5), custom_call_target="InvertDiagBlocksLowerTriangular" | custom-call | tf_op jit(solution)/shard_map/jit(_solve_triangular)/triangular_solve | solution.py:15
  247.6 0.3 fusion.3
  248.0 2.4 fusion.20
  250.3 0.3 fusion.21
  250.6 0.1 copy.137
  250.7 6.0 %cholesky.70 = f32[64,64]{1,0:T(8,128)S(1)} custom-call(f32[64,64]{1,0:T(8,128)S(1)} %fusion.11), custom_call_target="Cholesky" | custom-call | tf_op jit(solution)/shard_map/jit(cholesky)/cholesky | solution.py:10
  256.7 0.6 compare_reduce_fusion.1
  257.4 0.7 fusion.6
  258.0 4.9 %custom-call.8 = f32[1,64,64]{1,2,0:T(8,128)S(1)} custom-call(f32[1,64,64]{2,1,0:T(8,128)S(1)} %fusion.6), custom_call_target="InvertDiagBlocksLowerTriangular" | custom-call | tf_op jit(solution)/shard_map/jit(_solve_triangular)/triangular_solve | solution.py:15
  262.9 0.3 fusion.1
  263.3 1.1 fusion.22
  264.4 0.3 fusion.23
  264.7 0.1 copy.138
  264.8 5.8 %cholesky.81 = f32[64,64]{1,0:T(8,128)S(1)} custom-call(f32[64,64]{1,0:T(8,128)S(1)} %fusion.9), custom_call_target="Cholesky" | custom-call | tf_op jit(solution)/shard_map/jit(cholesky)/cholesky | solution.py:10
  270.7 0.6 compare_reduce_fusion
  271.3 0.7 fusion.7
  272.0 4.9 %custom-call.9 = f32[1,64,64]{1,2,0:T(8,128)S(1)} custom-call(f32[1,64,64]{2,1,0:T(8,128)S(1)} %fusion.7), custom_call_target="InvertDiagBlocksLowerTriangular" | custom-call | tf_op jit(solution)/shard_map/jit(_solve_triangular)/triangular_solve | solution.py:15
  276.9 0.3 convolution_bitcast_fusion.2
  277.2 5.6 %convolution_bitcast_fusion.1 = f32[2,8,64,128]{3,2,1,0:T(8,128)} fusion(f32[64,512,1,1]{1,0,3,2:T(8,128)S(1)} %convolution_bitcast_fusion.2, f32[2,512,8,128]{3,1,2,0:T(8,128)} %bitcast.581), kind=kOutput, calls=%fused_computation.1 | convolution fusion | flops 805306368 | bytes 4849664 | tf_op jit(solution)/shard_map/fzxy,zk->fxky/dot_general | solution.py:52
  (140 shorter events, 1.5 us)
Async XLA Ops:
  6.5 226.2 %copy-start = (f32[512,64]{0,1:T(8,128)S(1)}, f32[512,64]{0,1:T(8,128)}, u32[]{:S(2)}) copy-start(f32[512,64]{0,1:T(8,128)} %param.6) | copy-start | bytes 393220
  6.5 226.2 %all-reduce.2.cloned.1.call-start = ((), (), s32[]{:S(2)}) async-start(), calls=%async_computation.1 | async-start | bytes 2097152 | tf_op jit(solution)/shard_map/psum | solution.py:41
  78.5 1.9 copy-start.1
  232.7 30.5 %copy-start.2 = (f32[512,512]{1,0:T(8,128)S(1)}, f32[512,512]{1,0:T(8,128)}, u32[]{:S(2)}) copy-start(f32[512,512]{1,0:T(8,128)} %all-reduce.2.cloned.1.call-done) | copy-start | bytes 3145732
Sparse Core Ops, SparseCore 0:
  88.5 144.2 all-reduce.1
